TPU v7x, 32 devices: a whole 2x2x4 slice. The times are simulated.
32 devices in a mesh: row: 8 (over z, y), col: 4 (over x, core).
Axes of the slice: x: 2, y: 2, z: 4, core: 2. Of those that a mesh axis runs over, the one named last changes fastest.
Arguments:
- rhs: float32 [32768, 256], P(('row', 'col')), may hold values from -6 to 6
- local_mat: bfloat16 [32768, 1024], P(('row', 'col')), may hold values from -1 to 5
- local_inv: bfloat16 [32768, 1024], P(('row', 'col')), may hold values from -1 to 1
- basis_t: bfloat16 [3072, 1024], P(('row', 'col')), may hold values from -0.1875 to 0.1875
- coarse_inv: bfloat16 [3072, 3072], P('col', 'row'), may hold values from -0.109375 to 0.109375
- couple: float32 [32, 4, 128], P(('row', 'col')), may hold values from 0.5 to 2
- margin_rows: int32 [32, 4, 128], P(('row', 'col')), may hold values from 0 to 1023, as said below
Outputs:
- solution: float32 [32768, 256], P(('row', 'col'))
- residual: float32 [32768, 256], P(('row', 'col'))
Inputs may be any that keep to these rules, and one draw needn't show every extreme that they name: `margin_rows`: within each subdomain the 512 listed rows are all different.
All inputs are finite; a program needn't handle non-finite values.
Results may differ from a plain program's by a relative error of at most 0.024.
Values may be sent and summed in bfloat16 or wider, within the bound.
No kernel may reach another device: no remote copies, remote signals or barrier semaphores. Data moves between devices by JAX's collectives and lax.ppermute only.
A program may use at most 64 MiB of HBM per device.

v0:
```python
import jax
import jax.numpy as jnp
from jax import lax
from jax.sharding import PartitionSpec as P

STEPS = 2


def padded(cells, sides, width):
    for axis, dim in sides:
        count = lax.axis_size(axis)
        ends = count - 1
        head = lax.slice_in_dim(cells, 0, width, axis=dim)
        tail = lax.slice_in_dim(cells, cells.shape[dim] - width, cells.shape[dim], axis=dim)
        cells = jnp.concatenate(
            [
                lax.ppermute(tail, axis, [(i, (i + 1) % count) for i in range(ends)]),
                cells,
                lax.ppermute(head, axis, [((i + 1) % count, i) for i in range(ends)]),
            ],
            axis=dim,
        )
    return cells


def per_device(rhs, local_mat, local_inv, basis_t, coarse_inv, couple, margin_rows):
    face_index = margin_rows[0]
    flat_rows = face_index.reshape(-1)
    weights = couple[0]
    columns = rhs.shape[1]

    def neighbour_faces(vector_b):
        face_vals = vector_b[face_index]
        north_south = padded(face_vals[0:2], (("row", 0),), 1)
        west_east = padded(face_vals[2:4], (("col", 0),), 1)
        received = jnp.stack([north_south[0], north_south[3], west_east[0], west_east[3]])
        return received

    def apply_operator(vector):
        vector_b = vector.astype(jnp.bfloat16)
        received = neighbour_faces(vector_b)
        coupling_terms = (weights[:, :, None] * received.astype(jnp.float32)).reshape(-1, columns)
        coupled = jnp.zeros(vector.shape, jnp.float32).at[flat_rows].add(coupling_terms)
        return jnp.dot(local_mat, vector_b, preferred_element_type=jnp.float32) - coupled

    solution = jnp.zeros(rhs.shape, jnp.float32)
    residual = rhs
    for sweep in range(STEPS):
        if sweep > 0:
            residual = rhs - apply_operator(solution)
        rounded = residual.astype(jnp.bfloat16)
        restricted = jnp.dot(basis_t, rounded, preferred_element_type=jnp.float32).astype(
            jnp.bfloat16
        )
        block_rows = restricted.shape[0]
        partial_sum = jnp.dot(
            coarse_inv,
            lax.all_gather(restricted, "col", axis=0, tiled=True),
            preferred_element_type=jnp.float32,
        )
        summed = lax.psum(partial_sum, "row")
        coarse_part = lax.dynamic_slice_in_dim(
            summed, lax.axis_index("row") * block_rows, block_rows, 0
        )
        coarse_b = coarse_part.astype(jnp.bfloat16)
        solution = solution + lax.dot_general(
            basis_t, coarse_b, (((0,), (0,)), ((), ())), preferred_element_type=jnp.float32
        )
        residual = rhs - apply_operator(solution)
        solution = solution + jnp.dot(
            local_inv, residual.astype(jnp.bfloat16), preferred_element_type=jnp.float32
        )
    residual = rhs - apply_operator(solution)
    return (solution, residual)


def solution(mesh):
    placed = (
        P(("row", "col"), None),
        P(("row", "col"), None),
        P(("row", "col"), None),
        P(("row", "col"), None),
        P("col", "row"),
        P(("row", "col"), None, None),
        P(("row", "col"), None, None),
    )
    return jax.shard_map(
        per_device,
        mesh=mesh,
        in_specs=placed,
        out_specs=(P(("row", "col"), None), P(("row", "col"), None)),
        check_vma=False,
    )
```

profile of v0, /device:TPU:9, one launch (start us, length us, event | category | flops | bytes accessed | tf_op | source)
XLA Modules:
  0.0 242.6 jit_solution(8589869174017089495)
XLA Ops:
  3.1 6.1 %all_gather.6 = bf16[384,256]{1,0:T(8,128)(2,1)S(1)} all-gather(bf16[96,256]{1,0:T(8,128)(2,1)S(1)} %convolution_convert_fusion), channel_id=1, replica_groups=mesh['row'=8,'col'=4] {'col'}, dimensions={0}, use_global_device_ids=true | all-gather | bytes 245760 | tf_op jit(solution)/shard_map/all_gather | solution.py:58
  10.7 40.2 %all-reduce.2 = bf16[768,256]{0,1:T(8,128)(2,1)} all-reduce(f32[768,256]{0,1:T(8,128)S(1)} %convolution_bitcast_fusion.5), channel_id=1, replica_groups=mesh['row'=8,'col'=4] {'row'}, use_global_device_ids=true, to_apply=%region_0.0 | all-reduce | flops 196608 | bytes 1179648 | tf_op jit(solution)/shard_map/psum | solution.py:61
  57.9 8.7 %collective-permute-start.2 = (bf16[1,128,256]{2,1,0:T(8,128)(2,1)}, bf16[1,128,256]{2,1,0:T(8,128)(2,1)}, u32[]{:S(2)}, u32[]{:S(2)}) collective-permute-start(bf16[1,128,256]{2,1,0:T(8,128)(2,1)} %get-tuple-element.21), channel_id=1, source_target_pairs={{0,1},{1,2},{2,3},{4,5},{5,6},{6,7},{8,9},{9,10},{10,11},{12,13},{... | collective-permute-start | bytes 196616 | tf_op jit(solution)/shard_map/ppermute | solution.py:17
  66.6 3.3 %collective-permute-start.1 = (bf16[1,128,256]{2,1,0:T(8,128)(2,1)S(1)}, bf16[1,128,256]{2,1,0:T(8,128)(2,1)}, u32[]{:S(2)}, u32[]{:S(2)}) collective-permute-start(bf16[1,128,256]{2,1,0:T(8,128)(2,1)S(1)} %get-tuple-element.22), channel_id=1, source_target_pairs={{4,0},{8,4},{12,8},{16,12},{20,16},{24,20},{28,24},{5,1},{9,5},{13... | collective-permute-start | bytes 196616 | tf_op jit(solution)/shard_map/ppermute | solution.py:19
  77.3 4.8 %scatter_custom_fusion = f32[1024,256]{1,0:T(8,128)} fusion(s32[512]{0:T(512)S(1)} %bitcast.127, bf16[512,256]{1,0:T(8,128)(2,1)} %bitcast.119, f32[]{:T(128)} %constant.4.clone.1, f32[512]{0:T(512)S(1)} %bitcast.122), kind=kCustom, calls=%fused_computation.40 | custom fusion | flops 393216 | bytes 1312772 | tf_op jit(solution)/shard_map/scatter-add | solution.py:43
  84.6 4.8 %convolution_add_fusion.2 = f32[256,1024]{1,0:T(8,128)} fusion(f32[256,1024]{1,0:T(8,128)} %copy-done.2, bf16[1024,1024]{1,0:T(8,128)(2,1)} %param.9, f32[1024,256]{0,1:T(8,128)S(1)} %copy.33, f32[1024,256]{0,1:T(8,128)} %copy.32, bf16[1024,1024]{1,0:T(8,128)(2,1)S(1)} %copy-done), kind=kOutput, calls=%fused_computation.23 | convolution fusion | flops 1075052544 | bytes 8388608 | tf_op jit(solution)/shard_map/dot_general | solution.py:70
  93.5 3.3 %gather_fusion.1 = bf16[512,256]{1,0:T(8,128)(2,1)} fusion(bf16[1024,256]{1,0:T(8,128)(2,1)} %copy.34, s32[1024]{0:T(1024)S(1)} %pad_clamp_fusion), kind=kCustom, calls=%fused_computation.1 | custom fusion | bytes 526336 | tf_op jit(solution)/shard_map/gather | solution.py:33
  101.8 4.2 %collective-permute-start.5 = (bf16[1,128,256]{2,1,0:T(8,128)(2,1)S(1)}, bf16[1,128,256]{2,1,0:T(8,128)(2,1)S(1)}, u32[]{:S(2)}, u32[]{:S(2)}) collective-permute-start(bf16[1,128,256]{2,1,0:T(8,128)(2,1)S(1)} %get-tuple-element.18), channel_id=1, source_target_pairs={{4,0},{8,4},{12,8},{16,12},{20,16},{24,20},{28,24},{5,1},{9,5},{13... | collective-permute-start | bytes 196616 | tf_op jit(solution)/shard_map/ppermute | solution.py:19
  106.0 2.6 %collective-permute-start.7 = (bf16[1,128,256]{2,1,0:T(8,128)(2,1)S(1)}, bf16[1,128,256]{2,1,0:T(8,128)(2,1)S(1)}, u32[]{:S(2)}, u32[]{:S(2)}) collective-permute-start(bf16[1,128,256]{2,1,0:T(8,128)(2,1)S(1)} %get-tuple-element.19), channel_id=1, source_target_pairs={{1,0},{2,1},{3,2},{5,4},{6,5},{7,6},{9,8},{10,9},{11,10},{13,12},{... | collective-permute-start | bytes 196616 | tf_op jit(solution)/shard_map/ppermute | solution.py:19
  108.6 3.0 %collective-permute-done.7 = bf16[1,128,256]{2,1,0:T(8,128)(2,1)S(1)} collective-permute-done((bf16[1,128,256]{2,1,0:T(8,128)(2,1)S(1)}, bf16[1,128,256]{2,1,0:T(8,128)(2,1)S(1)}, u32[]{:S(2)}, u32[]{:S(2)}) %collective-permute-start.7) | collective-permute-done | bytes 65568 | tf_op jit(solution)/shard_map/ppermute | solution.py:19
  112.3 4.8 %scatter_custom_fusion.1 = f32[1024,256]{1,0:T(8,128)} fusion(s32[512]{0:T(512)S(1)} %bitcast.128, bf16[512,256]{1,0:T(8,128)(2,1)} %bitcast.120, f32[]{:T(128)} %constant.4.clone.1, f32[512]{0:T(512)S(1)} %bitcast.123), kind=kCustom, calls=%fused_computation.38 | custom fusion | flops 393216 | bytes 1312772 | tf_op jit(solution)/shard_map/scatter-add | solution.py:43
  122.2 4.4 %all_gather.7 = bf16[384,256]{1,0:T(8,128)(2,1)S(1)} all-gather(bf16[96,256]{1,0:T(8,128)(2,1)S(1)} %fusion.14), channel_id=1, replica_groups=mesh['row'=8,'col'=4] {'col'}, dimensions={0}, use_global_device_ids=true | all-gather | bytes 245760 | tf_op jit(solution)/shard_map/all_gather | solution.py:58
  129.0 39.4 %all-reduce.3 = bf16[768,256]{0,1:T(8,128)(2,1)} all-reduce(f32[768,256]{0,1:T(8,128)} %convolution_bitcast_fusion.4), channel_id=1, replica_groups=mesh['row'=8,'col'=4] {'row'}, use_global_device_ids=true, to_apply=%region_3.0 | all-reduce | flops 196608 | bytes 1179648 | tf_op jit(solution)/shard_map/psum | solution.py:61
  173.9 2.7 %gather_fusion.2 = bf16[512,256]{1,0:T(8,128)(2,1)S(1)} fusion(bf16[1024,256]{1,0:T(8,128)(2,1)} %copy.37, s32[1024]{0:T(1024)S(1)} %pad_clamp_fusion), kind=kCustom, calls=%fused_computation.2 | custom fusion | bytes 526336 | tf_op jit(solution)/shard_map/gather | solution.py:33
  178.6 8.4 %collective-permute-start.10 = (bf16[1,128,256]{2,1,0:T(8,128)(2,1)S(1)}, bf16[1,128,256]{2,1,0:T(8,128)(2,1)S(1)}, u32[]{:S(2)}, u32[]{:S(2)}) collective-permute-start(bf16[1,128,256]{2,1,0:T(8,128)(2,1)S(1)} %get-tuple-element.13), channel_id=1, source_target_pairs={{0,1},{1,2},{2,3},{4,5},{5,6},{6,7},{8,9},{9,10},{10,11},{12,13},{... | collective-permute-start | bytes 196616 | tf_op jit(solution)/shard_map/ppermute | solution.py:17
  187.0 4.5 %collective-permute-start.9 = (bf16[1,128,256]{2,1,0:T(8,128)(2,1)S(1)}, bf16[1,128,256]{2,1,0:T(8,128)(2,1)S(1)}, u32[]{:S(2)}, u32[]{:S(2)}) collective-permute-start(bf16[1,128,256]{2,1,0:T(8,128)(2,1)S(1)} %get-tuple-element.14), channel_id=1, source_target_pairs={{4,0},{8,4},{12,8},{16,12},{20,16},{24,20},{28,24},{5,1},{9,5},{13... | collective-permute-start | bytes 196616 | tf_op jit(solution)/shard_map/ppermute | solution.py:19
  193.5 3.6 %collective-permute-done.11 = bf16[1,128,256]{2,1,0:T(8,128)(2,1)S(1)} collective-permute-done((bf16[1,128,256]{2,1,0:T(8,128)(2,1)S(1)}, bf16[1,128,256]{2,1,0:T(8,128)(2,1)S(1)}, u32[]{:S(2)}, u32[]{:S(2)}) %collective-permute-start.11) | collective-permute-done | bytes 65568 | tf_op jit(solution)/shard_map/ppermute | solution.py:19
  197.2 4.4 %scatter_custom_fusion.2 = f32[1024,256]{1,0:T(8,128)} fusion(s32[512]{0:T(512)S(1)} %bitcast.129, bf16[512,256]{1,0:T(8,128)(2,1)S(1)} %bitcast.121, f32[]{:T(128)} %constant.4.clone.1, f32[512]{0:T(512)S(1)} %bitcast.124), kind=kCustom, calls=%fused_computation.36 | custom fusion | flops 393216 | bytes 1312772 | tf_op jit(solution)/shard_map/scatter-add | solution.py:43
  201.6 2.6 %copy.38 = f32[1024,256]{0,1:T(8,128)} copy(f32[1024,256]{1,0:T(8,128)} %scatter_custom_fusion.2) | data formatting | bytes 2097152 | tf_op jit(solution)/shard_map/scatter-add | solution.py:43
  204.2 5.0 %fusion.38 = (bf16[1024,256]{0,1:T(8,128)(2,1)}, f32[1024,256]{0,1:T(8,128)}) fusion(f32[256,1024]{1,0:T(8,128)} %copy-done.1, bf16[1024,1024]{1,0:T(8,128)(2,1)} %param.9, f32[1024,256]{0,1:T(8,128)S(1)} %copy.33, f32[1024,256]{0,1:T(8,128)} %copy.38, bf16[1024,1024]{1,0:T(8,128)(2,1)S(1)} %copy-done), kind=kOutput, calls=%fused_computation.85 | convolution fusion | flops 1075314688 | bytes 8912896 | tf_op jit(solution)/shard_map/dot_general | solution.py:70
  211.2 2.7 %gather_fusion.3 = bf16[512,256]{1,0:T(8,128)(2,1)S(1)} fusion(bf16[1024,256]{1,0:T(8,128)(2,1)} %copy.40, s32[1024]{0:T(1024)S(1)} %pad_clamp_fusion), kind=kCustom, calls=%fused_computation.3 | custom fusion | bytes 526336 | tf_op jit(solution)/shard_map/gather | solution.py:33
  218.3 4.5 %collective-permute-start.13 = (bf16[1,128,256]{2,1,0:T(8,128)(2,1)}, bf16[1,128,256]{2,1,0:T(8,128)(2,1)S(1)}, u32[]{:S(2)}, u32[]{:S(2)}) collective-permute-start(bf16[1,128,256]{2,1,0:T(8,128)(2,1)} %get-tuple-element.10), channel_id=1, source_target_pairs={{4,0},{8,4},{12,8},{16,12},{20,16},{24,20},{28,24},{5,1},{9,5},{13... | collective-permute-start | bytes 196616 | tf_op jit(solution)/shard_map/ppermute | solution.py:19
  230.0 4.4 %scatter_custom_fusion.3 = f32[1024,256]{1,0:T(8,128)} fusion(s32[512]{0:T(512)S(1)} %bitcast.130, bf16[512,256]{1,0:T(8,128)(2,1)S(1)} %bitcast.118, f32[]{:T(128)} %constant.4.clone.1, f32[512]{0:T(512)S(1)} %bitcast.125), kind=kCustom, calls=%fused_computation.34 | custom fusion | flops 393216 | bytes 1312772 | tf_op jit(solution)/shard_map/scatter-add | solution.py:43
  237.0 3.1 %fusion.7 = f32[1024,256]{0,1:T(8,128)} fusion(f32[1024,256]{0,1:T(8,128)S(1)} %copy.33, f32[1024,256]{0,1:T(8,128)} %copy.41, bf16[1024,256]{0,1:T(8,128)(2,1)} %get-tuple-element.24, bf16[1024,1024]{1,0:T(8,128)(2,1)S(1)} %copy-done), kind=kOutput, calls=%fused_computation.20 | convolution fusion | flops 537395200 | bytes 5767168 | tf_op jit(solution)/shard_map/dot_general | solution.py:44
  (70 shorter events, 66.1 us)
Async XLA Ops:
  0.6 84.0 %copy-start = (bf16[1024,1024]{1,0:T(8,128)(2,1)S(1)}, bf16[1024,1024]{1,0:T(8,128)(2,1)}, u32[]{:S(2)}) copy-start(bf16[1024,1024]{1,0:T(8,128)(2,1)} %param.8) | copy-start | bytes 6291460
  1.5 49.4 %copy-start.3 = (bf16[96,1024]{1,0:T(8,128)(2,1)S(1)}, bf16[96,1024]{1,0:T(8,128)(2,1)}, u32[]{:S(2)}) copy-start(bf16[96,1024]{1,0:T(8,128)(2,1)} %param.10) | copy-start | bytes 589828
  52.1 1.0 copy-start.2
  53.1 18.7 %copy-start.7 = (s32[1,4,128]{2,1,0:T(4,128)S(1)}, s32[1,4,128]{2,1,0:T(4,128)}, u32[]{:S(2)}) copy-start(s32[1,4,128]{2,1,0:T(4,128)} %param.13) | copy-start | bytes 6148
  55.3 21.9 %copy-start.6 = (f32[1,4,128]{2,1,0:T(4,128)S(1)}, f32[1,4,128]{2,1,0:T(4,128)}, u32[]{:S(2)}) copy-start(f32[1,4,128]{2,1,0:T(4,128)} %param.12) | copy-start | bytes 6148
  56.0 17.5 %collective-permute-start = (bf16[1,128,256]{2,1,0:T(8,128)(2,1)}, bf16[1,128,256]{2,1,0:T(8,128)(2,1)S(1)}, u32[]{:S(2)}, u32[]{:S(2)}) collective-permute-start(bf16[1,128,256]{2,1,0:T(8,128)(2,1)} %get-tuple-element.20), channel_id=1, source_target_pairs={{0,4},{4,8},{8,12},{12,16},{16,20},{20,24},{24,28},{1,5},{5,9},{9,... | collective-permute-start | bytes 196616 | tf_op jit(solution)/shard_map/ppermute | solution.py:17
  57.9 15.6 %collective-permute-start.2 = (bf16[1,128,256]{2,1,0:T(8,128)(2,1)}, bf16[1,128,256]{2,1,0:T(8,128)(2,1)}, u32[]{:S(2)}, u32[]{:S(2)}) collective-permute-start(bf16[1,128,256]{2,1,0:T(8,128)(2,1)} %get-tuple-element.21), channel_id=1, source_target_pairs={{0,1},{1,2},{2,3},{4,5},{5,6},{6,7},{8,9},{9,10},{10,11},{12,13},{... | collective-permute-start | bytes 196616 | tf_op jit(solution)/shard_map/ppermute | solution.py:17
  66.6 6.9 %collective-permute-start.1 = (bf16[1,128,256]{2,1,0:T(8,128)(2,1)S(1)}, bf16[1,128,256]{2,1,0:T(8,128)(2,1)}, u32[]{:S(2)}, u32[]{:S(2)}) collective-permute-start(bf16[1,128,256]{2,1,0:T(8,128)(2,1)S(1)} %get-tuple-element.22), channel_id=1, source_target_pairs={{4,0},{8,4},{12,8},{16,12},{20,16},{24,20},{28,24},{5,1},{9,5},{13... | collective-permute-start | bytes 196616 | tf_op jit(solution)/shard_map/ppermute | solution.py:19
  69.9 5.7 %collective-permute-start.3 = (bf16[1,128,256]{2,1,0:T(8,128)(2,1)S(1)}, bf16[1,128,256]{2,1,0:T(8,128)(2,1)}, u32[]{:S(2)}, u32[]{:S(2)}) collective-permute-start(bf16[1,128,256]{2,1,0:T(8,128)(2,1)S(1)} %get-tuple-element.23), channel_id=1, source_target_pairs={{1,0},{2,1},{3,2},{5,4},{6,5},{7,6},{9,8},{10,9},{11,10},{13,12},{... | collective-permute-start | bytes 196616 | tf_op jit(solution)/shard_map/ppermute | solution.py:19
  97.8 10.8 %collective-permute-start.4 = (bf16[1,128,256]{2,1,0:T(8,128)(2,1)S(1)}, bf16[1,128,256]{2,1,0:T(8,128)(2,1)S(1)}, u32[]{:S(2)}, u32[]{:S(2)}) collective-permute-start(bf16[1,128,256]{2,1,0:T(8,128)(2,1)S(1)} %get-tuple-element.16), channel_id=1, source_target_pairs={{0,4},{4,8},{8,12},{12,16},{16,20},{20,24},{24,28},{1,5},{5,9},{9,... | collective-permute-start | bytes 196616 | tf_op jit(solution)/shard_map/ppermute | solution.py:17
  99.7 8.9 %collective-permute-start.6 = (bf16[1,128,256]{2,1,0:T(8,128)(2,1)S(1)}, bf16[1,128,256]{2,1,0:T(8,128)(2,1)S(1)}, u32[]{:S(2)}, u32[]{:S(2)}) collective-permute-start(bf16[1,128,256]{2,1,0:T(8,128)(2,1)S(1)} %get-tuple-element.17), channel_id=1, source_target_pairs={{0,1},{1,2},{2,3},{4,5},{5,6},{6,7},{8,9},{9,10},{10,11},{12,13},{... | collective-permute-start | bytes 196616 | tf_op jit(solution)/shard_map/ppermute | solution.py:17
  101.8 6.8 %collective-permute-start.5 = (bf16[1,128,256]{2,1,0:T(8,128)(2,1)S(1)}, bf16[1,128,256]{2,1,0:T(8,128)(2,1)S(1)}, u32[]{:S(2)}, u32[]{:S(2)}) collective-permute-start(bf16[1,128,256]{2,1,0:T(8,128)(2,1)S(1)} %get-tuple-element.18), channel_id=1, source_target_pairs={{4,0},{8,4},{12,8},{16,12},{20,16},{24,20},{28,24},{5,1},{9,5},{13... | collective-permute-start | bytes 196616 | tf_op jit(solution)/shard_map/ppermute | solution.py:19
  106.0 5.6 %collective-permute-start.7 = (bf16[1,128,256]{2,1,0:T(8,128)(2,1)S(1)}, bf16[1,128,256]{2,1,0:T(8,128)(2,1)S(1)}, u32[]{:S(2)}, u32[]{:S(2)}) collective-permute-start(bf16[1,128,256]{2,1,0:T(8,128)(2,1)S(1)} %get-tuple-element.19), channel_id=1, source_target_pairs={{1,0},{2,1},{3,2},{5,4},{6,5},{7,6},{9,8},{10,9},{11,10},{13,12},{... | collective-permute-start | bytes 196616 | tf_op jit(solution)/shard_map/ppermute | solution.py:19
  170.0 1.0 copy-start.1
  176.6 16.8 %collective-permute-start.8 = (bf16[1,128,256]{2,1,0:T(8,128)(2,1)S(1)}, bf16[1,128,256]{2,1,0:T(8,128)(2,1)S(1)}, u32[]{:S(2)}, u32[]{:S(2)}) collective-permute-start(bf16[1,128,256]{2,1,0:T(8,128)(2,1)S(1)} %get-tuple-element.12), channel_id=1, source_target_pairs={{0,4},{4,8},{8,12},{12,16},{16,20},{20,24},{24,28},{1,5},{5,9},{9,... | collective-permute-start | bytes 196616 | tf_op jit(solution)/shard_map/ppermute | solution.py:17
  178.6 14.9 %collective-permute-start.10 = (bf16[1,128,256]{2,1,0:T(8,128)(2,1)S(1)}, bf16[1,128,256]{2,1,0:T(8,128)(2,1)S(1)}, u32[]{:S(2)}, u32[]{:S(2)}) collective-permute-start(bf16[1,128,256]{2,1,0:T(8,128)(2,1)S(1)} %get-tuple-element.13), channel_id=1, source_target_pairs={{0,1},{1,2},{2,3},{4,5},{5,6},{6,7},{8,9},{9,10},{10,11},{12,13},{... | collective-permute-start | bytes 196616 | tf_op jit(solution)/shard_map/ppermute | solution.py:17
  187.0 6.5 %collective-permute-start.9 = (bf16[1,128,256]{2,1,0:T(8,128)(2,1)S(1)}, bf16[1,128,256]{2,1,0:T(8,128)(2,1)S(1)}, u32[]{:S(2)}, u32[]{:S(2)}) collective-permute-start(bf16[1,128,256]{2,1,0:T(8,128)(2,1)S(1)} %get-tuple-element.14), channel_id=1, source_target_pairs={{4,0},{8,4},{12,8},{16,12},{20,16},{24,20},{28,24},{5,1},{9,5},{13... | collective-permute-start | bytes 196616 | tf_op jit(solution)/shard_map/ppermute | solution.py:19
  191.5 5.6 %collective-permute-start.11 = (bf16[1,128,256]{2,1,0:T(8,128)(2,1)S(1)}, bf16[1,128,256]{2,1,0:T(8,128)(2,1)S(1)}, u32[]{:S(2)}, u32[]{:S(2)}) collective-permute-start(bf16[1,128,256]{2,1,0:T(8,128)(2,1)S(1)} %get-tuple-element.15), channel_id=1, source_target_pairs={{1,0},{2,1},{3,2},{5,4},{6,5},{7,6},{9,8},{10,9},{11,10},{13,12},{... | collective-permute-start | bytes 196616 | tf_op jit(solution)/shard_map/ppermute | solution.py:19
  214.5 13.3 %collective-permute-start.12 = (bf16[1,128,256]{2,1,0:T(8,128)(2,1)}, bf16[1,128,256]{2,1,0:T(8,128)(2,1)S(1)}, u32[]{:S(2)}, u32[]{:S(2)}) collective-permute-start(bf16[1,128,256]{2,1,0:T(8,128)(2,1)} %get-tuple-element.8), channel_id=1, source_target_pairs={{0,4},{4,8},{8,12},{12,16},{16,20},{20,24},{24,28},{1,5},{5,9},{9,... | collective-permute-start | bytes 196616 | tf_op jit(solution)/shard_map/ppermute | solution.py:17
  216.4 11.4 %collective-permute-start.14 = (bf16[1,128,256]{2,1,0:T(8,128)(2,1)}, bf16[1,128,256]{2,1,0:T(8,128)(2,1)S(1)}, u32[]{:S(2)}, u32[]{:S(2)}) collective-permute-start(bf16[1,128,256]{2,1,0:T(8,128)(2,1)} %get-tuple-element.9), channel_id=1, source_target_pairs={{0,1},{1,2},{2,3},{4,5},{5,6},{6,7},{8,9},{9,10},{10,11},{12,13},{... | collective-permute-start | bytes 196616 | tf_op jit(solution)/shard_map/ppermute | solution.py:17
  218.3 9.5 %collective-permute-start.13 = (bf16[1,128,256]{2,1,0:T(8,128)(2,1)}, bf16[1,128,256]{2,1,0:T(8,128)(2,1)S(1)}, u32[]{:S(2)}, u32[]{:S(2)}) collective-permute-start(bf16[1,128,256]{2,1,0:T(8,128)(2,1)} %get-tuple-element.10), channel_id=1, source_target_pairs={{4,0},{8,4},{12,8},{16,12},{20,16},{24,20},{28,24},{5,1},{9,5},{13... | collective-permute-start | bytes 196616 | tf_op jit(solution)/shard_map/ppermute | solution.py:19
  222.8 6.2 %collective-permute-start.15 = (bf16[1,128,256]{2,1,0:T(8,128)(2,1)S(1)}, bf16[1,128,256]{2,1,0:T(8,128)(2,1)}, u32[]{:S(2)}, u32[]{:S(2)}) collective-permute-start(bf16[1,128,256]{2,1,0:T(8,128)(2,1)S(1)} %get-tuple-element.11), channel_id=1, source_target_pairs={{1,0},{2,1},{3,2},{5,4},{6,5},{7,6},{9,8},{10,9},{11,10},{13,12},{... | collective-permute-start | bytes 196616 | tf_op jit(solution)/shard_map/ppermute | solution.py:19
  227.8 0.6 copy-start.4
  228.5 0.6 copy-start.5
where the time goes:
time: 244 us; the launch traced here: 243 us
  blocking collectives  90.2 us (37%)
  starting transfers between devices  54.2 us (22%)
  local copies, waits for them, and re-layouts  39.2 us (16%)
  other arithmetic  25.7 us (11%)
  matrix products  23.6 us (10%)
  waiting for transfers between devices  8.78 us (4%)
    psum x2, blocking collectives, per_device(): summed = lax.psum(partial_sum, 'row')  79.6 us
    ppermute x8, starting transfers between devices, padded(): lax.ppermute(tail, axis, [(i, (i + 1) % count) for i in range(ends)])  28.7 us
    ppermute x8, starting transfers between devices, padded(): lax.ppermute(head, axis, [((i + 1) % count, i) for i in range(ends)])  25.5 us
    scatter-add x4, other arithmetic, apply_operator(): jnp.zeros(vector.shape, jnp.float32).at[flat_rows].add(coupling_terms)  18.5 us
    gather x4, local copies, waits for them, and re-layouts, neighbour_faces(): face_vals = vector_b[face_index]  10.6 us
    all_gather x2, blocking collectives, per_device(): lax.all_gather(restricted, 'col', axis=0, tiled=True)  10.6 us
    scatter-add x4, local copies, waits for them, and re-layouts, apply_operator(): jnp.zeros(vector.shape, jnp.float32).at[flat_rows].add(coupling_terms)  10.2 us
    unnamed x19, local copies, waits for them, and re-layouts  9.8 us
  transfers between devices with their start and end apart: 16, of which 3 were waited for; matrix products, arithmetic and copies ran while one was open for 2% of the time, Pallas kernels for 0%

commit v1 on v0

--- a/solution.py
+++ b/solution.py
@@ -58,7 +58,9 @@
             lax.all_gather(restricted, "col", axis=0, tiled=True),
             preferred_element_type=jnp.float32,
         )
-        summed = lax.psum(partial_sum, "row")
+        summed = partial_sum
+        for hop in (1, 2, 4):
+            summed = summed + lax.ppermute(summed, "row", [(dev, dev ^ hop) for dev in range(8)])
         coarse_part = lax.dynamic_slice_in_dim(
             summed, lax.axis_index("row") * block_rows, block_rows, 0
         )

time: 244 us -> 302 us (1.24)
  waiting for transfers between devices: 8.78 us -> 148 us
  blocking collectives: 90.2 us -> 10.6 us
    ppermute x0 -> x6, waiting for transfers between devices: none -> 139 us  [per_device(): lax.ppermute(summed, 'row', [(dev, dev ^ hop) for dev in range(8)])]
    psum x2 -> x0, blocking collectives: 79.6 us -> none  [per_device(): summed = lax.psum(partial_sum, 'row')]
    ppermute x0 -> x6, starting transfers between devices: none -> 7.81 us  [per_device(): lax.ppermute(summed, 'row', [(dev, dev ^ hop) for dev in range(8)])]
    ppermute x8, starting transfers between devices: 28.7 us -> 21.6 us  [padded(): lax.ppermute(tail, axis, [(i, (i + 1) % count) for i in range(ends)])]
    unnamed x19 -> x21, local copies, waits for them, and re-layouts: 9.8 us -> 9.83 us
  transfers between devices with their start and end apart: 16 -> 22, of which waited for: 3 -> 9; matrix products, arithmetic and copies ran while one was open for 2% -> 1% of each run, Pallas kernels for 0% -> 0%
where the time goes in v1:
time: 302 us; the launch traced here: 300 us
  waiting for transfers between devices  148 us (49%)
  starting transfers between devices  54 us (18%)
  local copies, waits for them, and re-layouts  39.3 us (13%)
  other arithmetic  25.2 us (8%)
  matrix products  21.6 us (7%)
  blocking collectives  10.6 us (4%)
    ppermute x6, waiting for transfers between devices, per_device(): lax.ppermute(summed, 'row', [(dev, dev ^ hop) for dev in range(8)])  139 us
    ppermute x8, starting transfers between devices, padded(): lax.ppermute(head, axis, [((i + 1) % count, i) for i in range(ends)])  24.6 us
    ppermute x8, starting transfers between devices, padded(): lax.ppermute(tail, axis, [(i, (i + 1) % count) for i in range(ends)])  21.6 us
    scatter-add x4, other arithmetic, apply_operator(): jnp.zeros(vector.shape, jnp.float32).at[flat_rows].add(coupling_terms)  18.5 us
    gather x4, local copies, waits for them, and re-layouts, neighbour_faces(): face_vals = vector_b[face_index]  10.6 us
    all_gather x2, blocking collectives, per_device(): lax.all_gather(restricted, 'col', axis=0, tiled=True)  10.6 us
    scatter-add x4, local copies, waits for them, and re-layouts, apply_operator(): jnp.zeros(vector.shape, jnp.float32).at[flat_rows].add(coupling_terms)  10.2 us
    unnamed x21, local copies, waits for them, and re-layouts  9.83 us
  transfers between devices with their start and end apart: 22, of which 9 were waited for; matrix products, arithmetic and copies ran while one was open for 1% of the time, Pallas kernels for 0%

profile of v1, /device:TPU:9, one launch (start us, length us, event | category | flops | bytes accessed | tf_op | source)
XLA Modules:
  0.0 299.9 jit_solution(9948670978928591235)
XLA Ops:
  2.3 6.1 %all_gather.6 = bf16[384,256]{1,0:T(8,128)(2,1)S(1)} all-gather(bf16[96,256]{1,0:T(8,128)(2,1)S(1)} %convolution_convert_fusion), channel_id=1, replica_groups=mesh['row'=8,'col'=4] {'col'}, dimensions={0}, use_global_device_ids=true | all-gather | bytes 245760 | tf_op jit(solution)/shard_map/all_gather | solution.py:58
  11.2 17.7 %collective-permute-done = f32[768,256]{0,1:T(8,128)S(1)} collective-permute-done((f32[768,256]{0,1:T(8,128)S(1)}, f32[768,256]{0,1:T(8,128)S(1)}, u32[]{:S(2)}, u32[]{:S(2)}) %collective-permute-start) | collective-permute-done | bytes 786464 | tf_op jit(solution)/shard_map/ppermute | solution.py:63
  29.1 18.1 %collective-permute-done.1 = f32[768,256]{0,1:T(8,128)S(1)} collective-permute-done((f32[768,256]{0,1:T(8,128)S(1)}, f32[768,256]{0,1:T(8,128)S(1)}, u32[]{:S(2)}, u32[]{:S(2)}) %collective-permute-start.1) | collective-permute-done | bytes 786464 | tf_op jit(solution)/shard_map/ppermute | solution.py:63
  49.7 34.0 %collective-permute-done.2 = f32[768,256]{0,1:T(8,128)} collective-permute-done((f32[768,256]{0,1:T(8,128)S(1)}, f32[768,256]{0,1:T(8,128)}, u32[]{:S(2)}, u32[]{:S(2)}) %collective-permute-start.2) | collective-permute-done | bytes 786464 | tf_op jit(solution)/shard_map/ppermute | solution.py:63
  88.8 3.1 %collective-permute-start.3 = (bf16[1,128,256]{2,1,0:T(8,128)(2,1)}, bf16[1,128,256]{2,1,0:T(8,128)(2,1)S(1)}, u32[]{:S(2)}, u32[]{:S(2)}) collective-permute-start(bf16[1,128,256]{2,1,0:T(8,128)(2,1)} %get-tuple-element.20), channel_id=1, source_target_pairs={{0,4},{4,8},{8,12},{12,16},{16,20},{20,24},{24,28},{1,5},{5,9},{9,... | collective-permute-start | bytes 196616 | tf_op jit(solution)/shard_map/ppermute | solution.py:17
  92.0 3.8 %collective-permute-start.5 = (bf16[1,128,256]{2,1,0:T(8,128)(2,1)}, bf16[1,128,256]{2,1,0:T(8,128)(2,1)}, u32[]{:S(2)}, u32[]{:S(2)}) collective-permute-start(bf16[1,128,256]{2,1,0:T(8,128)(2,1)} %get-tuple-element.21), channel_id=1, source_target_pairs={{0,1},{1,2},{2,3},{4,5},{5,6},{6,7},{8,9},{9,10},{10,11},{12,13},{... | collective-permute-start | bytes 196616 | tf_op jit(solution)/shard_map/ppermute | solution.py:17
  106.2 4.8 %scatter_custom_fusion = f32[1024,256]{1,0:T(8,128)} fusion(s32[512]{0:T(512)S(1)} %bitcast.127, bf16[512,256]{1,0:T(8,128)(2,1)} %bitcast.119, f32[]{:T(128)} %constant.4.clone.1, f32[512]{0:T(512)S(1)} %bitcast.122), kind=kCustom, calls=%fused_computation.40 | custom fusion | flops 393216 | bytes 1312772 | tf_op jit(solution)/shard_map/scatter-add | solution.py:43
  113.5 4.8 %convolution_add_fusion.2 = f32[256,1024]{1,0:T(8,128)} fusion(f32[256,1024]{1,0:T(8,128)} %copy-done.3, bf16[1024,1024]{1,0:T(8,128)(2,1)} %param.9, f32[1024,256]{0,1:T(8,128)S(1)} %copy.33, f32[1024,256]{0,1:T(8,128)} %copy.32, bf16[1024,1024]{1,0:T(8,128)(2,1)S(1)} %copy-done), kind=kOutput, calls=%fused_computation.23 | convolution fusion | flops 1075052544 | bytes 8388608 | tf_op jit(solution)/shard_map/dot_general | solution.py:72
  122.5 3.3 %gather_fusion.1 = bf16[512,256]{1,0:T(8,128)(2,1)} fusion(bf16[1024,256]{1,0:T(8,128)(2,1)} %copy.34, s32[1024]{0:T(1024)S(1)} %pad_clamp_fusion), kind=kCustom, calls=%fused_computation.1 | custom fusion | bytes 526336 | tf_op jit(solution)/shard_map/gather | solution.py:33
  131.0 3.9 %collective-permute-start.8 = (bf16[1,128,256]{2,1,0:T(8,128)(2,1)S(1)}, bf16[1,128,256]{2,1,0:T(8,128)(2,1)S(1)}, u32[]{:S(2)}, u32[]{:S(2)}) collective-permute-start(bf16[1,128,256]{2,1,0:T(8,128)(2,1)S(1)} %get-tuple-element.18), channel_id=1, source_target_pairs={{4,0},{8,4},{12,8},{16,12},{20,16},{24,20},{28,24},{5,1},{9,5},{13... | collective-permute-start | bytes 196616 | tf_op jit(solution)/shard_map/ppermute | solution.py:19
  141.3 4.8 %scatter_custom_fusion.1 = f32[1024,256]{1,0:T(8,128)} fusion(s32[512]{0:T(512)S(1)} %bitcast.128, bf16[512,256]{1,0:T(8,128)(2,1)} %bitcast.120, f32[]{:T(128)} %constant.4.clone.1, f32[512]{0:T(512)S(1)} %bitcast.123), kind=kCustom, calls=%fused_computation.38 | custom fusion | flops 393216 | bytes 1312772 | tf_op jit(solution)/shard_map/scatter-add | solution.py:43
  151.2 4.4 %all_gather.7 = bf16[384,256]{1,0:T(8,128)(2,1)S(1)} all-gather(bf16[96,256]{1,0:T(8,128)(2,1)S(1)} %fusion.14), channel_id=1, replica_groups=mesh['row'=8,'col'=4] {'col'}, dimensions={0}, use_global_device_ids=true | all-gather | bytes 245760 | tf_op jit(solution)/shard_map/all_gather | solution.py:58
  157.2 18.7 %collective-permute-done.11 = f32[768,256]{0,1:T(8,128)S(1)} collective-permute-done((f32[768,256]{0,1:T(8,128)S(1)}, f32[768,256]{0,1:T(8,128)S(1)}, u32[]{:S(2)}, u32[]{:S(2)}) %collective-permute-start.11) | collective-permute-done | bytes 786464 | tf_op jit(solution)/shard_map/ppermute | solution.py:63
  176.7 17.2 %collective-permute-done.12 = f32[768,256]{0,1:T(8,128)S(1)} collective-permute-done((f32[768,256]{0,1:T(8,128)S(1)}, f32[768,256]{0,1:T(8,128)S(1)}, u32[]{:S(2)}, u32[]{:S(2)}) %collective-permute-start.12) | collective-permute-done | bytes 786464 | tf_op jit(solution)/shard_map/ppermute | solution.py:63
  194.1 3.3 %collective-permute-start.13 = (f32[768,256]{0,1:T(8,128)S(1)}, f32[768,256]{0,1:T(8,128)S(1)}, u32[]{:S(2)}, u32[]{:S(2)}) collective-permute-start(f32[768,256]{0,1:T(8,128)S(1)} %add.78), channel_id=1, source_target_pairs={{0,16},{4,20},{8,24},{12,28},{16,0},{20,4},{24,8},{28,12},{1,17},{... | collective-permute-start | bytes 2359304 | tf_op jit(solution)/shard_map/ppermute | solution.py:63
  197.3 33.6 %collective-permute-done.13 = f32[768,256]{0,1:T(8,128)S(1)} collective-permute-done((f32[768,256]{0,1:T(8,128)S(1)}, f32[768,256]{0,1:T(8,128)S(1)}, u32[]{:S(2)}, u32[]{:S(2)}) %collective-permute-start.13) | collective-permute-done | bytes 786464 | tf_op jit(solution)/shard_map/ppermute | solution.py:63
  239.8 4.7 %collective-permute-start.16 = (bf16[1,128,256]{2,1,0:T(8,128)(2,1)S(1)}, bf16[1,128,256]{2,1,0:T(8,128)(2,1)S(1)}, u32[]{:S(2)}, u32[]{:S(2)}) collective-permute-start(bf16[1,128,256]{2,1,0:T(8,128)(2,1)S(1)} %get-tuple-element.13), channel_id=1, source_target_pairs={{0,1},{1,2},{2,3},{4,5},{5,6},{6,7},{8,9},{9,10},{10,11},{12,13},{... | collective-permute-start | bytes 196616 | tf_op jit(solution)/shard_map/ppermute | solution.py:17
  244.5 4.3 %collective-permute-start.15 = (bf16[1,128,256]{2,1,0:T(8,128)(2,1)S(1)}, bf16[1,128,256]{2,1,0:T(8,128)(2,1)S(1)}, u32[]{:S(2)}, u32[]{:S(2)}) collective-permute-start(bf16[1,128,256]{2,1,0:T(8,128)(2,1)S(1)} %get-tuple-element.14), channel_id=1, source_target_pairs={{4,0},{8,4},{12,8},{16,12},{20,16},{24,20},{28,24},{5,1},{9,5},{13... | collective-permute-start | bytes 196616 | tf_op jit(solution)/shard_map/ppermute | solution.py:19
  250.7 3.6 %collective-permute-done.17 = bf16[1,128,256]{2,1,0:T(8,128)(2,1)S(1)} collective-permute-done((bf16[1,128,256]{2,1,0:T(8,128)(2,1)S(1)}, bf16[1,128,256]{2,1,0:T(8,128)(2,1)S(1)}, u32[]{:S(2)}, u32[]{:S(2)}) %collective-permute-start.17) | collective-permute-done | bytes 65568 | tf_op jit(solution)/shard_map/ppermute | solution.py:19
  254.4 4.4 %scatter_custom_fusion.2 = f32[1024,256]{1,0:T(8,128)} fusion(s32[512]{0:T(512)S(1)} %bitcast.129, bf16[512,256]{1,0:T(8,128)(2,1)S(1)} %bitcast.121, f32[]{:T(128)} %constant.4.clone.1, f32[512]{0:T(512)S(1)} %bitcast.124), kind=kCustom, calls=%fused_computation.36 | custom fusion | flops 393216 | bytes 1312772 | tf_op jit(solution)/shard_map/scatter-add | solution.py:43
  261.3 5.0 %fusion.42 = (bf16[1024,256]{0,1:T(8,128)(2,1)}, f32[1024,256]{0,1:T(8,128)}) fusion(f32[256,1024]{1,0:T(8,128)} %copy-done.1, bf16[1024,1024]{1,0:T(8,128)(2,1)} %param.9, f32[1024,256]{0,1:T(8,128)S(1)} %copy.33, f32[1024,256]{0,1:T(8,128)} %copy.38, bf16[1024,1024]{1,0:T(8,128)(2,1)S(1)} %copy-done), kind=kOutput, calls=%fused_computation.87 | convolution fusion | flops 1075314688 | bytes 8912896 | tf_op jit(solution)/shard_map/dot_general | solution.py:72
  275.5 4.5 %collective-permute-start.19 = (bf16[1,128,256]{2,1,0:T(8,128)(2,1)}, bf16[1,128,256]{2,1,0:T(8,128)(2,1)S(1)}, u32[]{:S(2)}, u32[]{:S(2)}) collective-permute-start(bf16[1,128,256]{2,1,0:T(8,128)(2,1)} %get-tuple-element.10), channel_id=1, source_target_pairs={{4,0},{8,4},{12,8},{16,12},{20,16},{24,20},{28,24},{5,1},{9,5},{13... | collective-permute-start | bytes 196616 | tf_op jit(solution)/shard_map/ppermute | solution.py:19
  287.2 4.4 %scatter_custom_fusion.3 = f32[1024,256]{1,0:T(8,128)} fusion(s32[512]{0:T(512)S(1)} %bitcast.130, bf16[512,256]{1,0:T(8,128)(2,1)S(1)} %bitcast.118, f32[]{:T(128)} %constant.4.clone.1, f32[512]{0:T(512)S(1)} %bitcast.125), kind=kCustom, calls=%fused_computation.34 | custom fusion | flops 393216 | bytes 1312772 | tf_op jit(solution)/shard_map/scatter-add | solution.py:43
  294.2 3.1 %fusion.7 = f32[1024,256]{0,1:T(8,128)} fusion(f32[1024,256]{0,1:T(8,128)S(1)} %copy.33, f32[1024,256]{0,1:T(8,128)} %copy.41, bf16[1024,256]{0,1:T(8,128)(2,1)} %get-tuple-element.24, bf16[1024,1024]{1,0:T(8,128)(2,1)S(1)} %copy-done), kind=kOutput, calls=%fused_computation.20 | convolution fusion | flops 537395200 | bytes 5767168 | tf_op jit(solution)/shard_map/dot_general | solution.py:44
  (86 shorter events, 83.2 us)
Async XLA Ops:
  0.6 112.9 %copy-start = (bf16[1024,1024]{1,0:T(8,128)(2,1)S(1)}, bf16[1024,1024]{1,0:T(8,128)(2,1)}, u32[]{:S(2)}) copy-start(bf16[1024,1024]{1,0:T(8,128)(2,1)} %param.8) | copy-start | bytes 6291460
  9.9 19.0 %collective-permute-start = (f32[768,256]{0,1:T(8,128)S(1)}, f32[768,256]{0,1:T(8,128)S(1)}, u32[]{:S(2)}, u32[]{:S(2)}) collective-permute-start(f32[768,256]{0,1:T(8,128)S(1)} %convolution_bitcast_fusion.5), channel_id=1, source_target_pairs={{0,4},{4,0},{8,12},{12,8},{16,20},{20,16},{24,28},{28,24},{1,5},{5... | collective-permute-start | bytes 2359304 | tf_op jit(solution)/shard_map/ppermute | solution.py:63
  29.0 18.1 %collective-permute-start.1 = (f32[768,256]{0,1:T(8,128)S(1)}, f32[768,256]{0,1:T(8,128)S(1)}, u32[]{:S(2)}, u32[]{:S(2)}) collective-permute-start(f32[768,256]{0,1:T(8,128)S(1)} %add.70), channel_id=1, source_target_pairs={{0,8},{4,12},{8,0},{12,4},{16,24},{20,28},{24,16},{28,20},{1,9},{5... | collective-permute-start | bytes 2359304 | tf_op jit(solution)/shard_map/ppermute | solution.py:63
  47.3 36.4 %collective-permute-start.2 = (f32[768,256]{0,1:T(8,128)S(1)}, f32[768,256]{0,1:T(8,128)}, u32[]{:S(2)}, u32[]{:S(2)}) collective-permute-start(f32[768,256]{0,1:T(8,128)S(1)} %add.71), channel_id=1, source_target_pairs={{0,16},{4,20},{8,24},{12,28},{16,0},{20,4},{24,8},{28,12},{1,17},{... | collective-permute-start | bytes 2359304 | tf_op jit(solution)/shard_map/ppermute | solution.py:63
  88.8 13.5 %collective-permute-start.3 = (bf16[1,128,256]{2,1,0:T(8,128)(2,1)}, bf16[1,128,256]{2,1,0:T(8,128)(2,1)S(1)}, u32[]{:S(2)}, u32[]{:S(2)}) collective-permute-start(bf16[1,128,256]{2,1,0:T(8,128)(2,1)} %get-tuple-element.20), channel_id=1, source_target_pairs={{0,4},{4,8},{8,12},{12,16},{16,20},{20,24},{24,28},{1,5},{5,9},{9,... | collective-permute-start | bytes 196616 | tf_op jit(solution)/shard_map/ppermute | solution.py:17
  92.0 10.4 %collective-permute-start.5 = (bf16[1,128,256]{2,1,0:T(8,128)(2,1)}, bf16[1,128,256]{2,1,0:T(8,128)(2,1)}, u32[]{:S(2)}, u32[]{:S(2)}) collective-permute-start(bf16[1,128,256]{2,1,0:T(8,128)(2,1)} %get-tuple-element.21), channel_id=1, source_target_pairs={{0,1},{1,2},{2,3},{4,5},{5,6},{6,7},{8,9},{9,10},{10,11},{12,13},{... | collective-permute-start | bytes 196616 | tf_op jit(solution)/shard_map/ppermute | solution.py:17
  95.8 6.6 %collective-permute-start.4 = (bf16[1,128,256]{2,1,0:T(8,128)(2,1)S(1)}, bf16[1,128,256]{2,1,0:T(8,128)(2,1)}, u32[]{:S(2)}, u32[]{:S(2)}) collective-permute-start(bf16[1,128,256]{2,1,0:T(8,128)(2,1)S(1)} %get-tuple-element.22), channel_id=1, source_target_pairs={{4,0},{8,4},{12,8},{16,12},{20,16},{24,20},{28,24},{5,1},{9,5},{13... | collective-permute-start | bytes 196616 | tf_op jit(solution)/shard_map/ppermute | solution.py:19
  98.8 5.7 %collective-permute-start.6 = (bf16[1,128,256]{2,1,0:T(8,128)(2,1)S(1)}, bf16[1,128,256]{2,1,0:T(8,128)(2,1)}, u32[]{:S(2)}, u32[]{:S(2)}) collective-permute-start(bf16[1,128,256]{2,1,0:T(8,128)(2,1)S(1)} %get-tuple-element.23), channel_id=1, source_target_pairs={{1,0},{2,1},{3,2},{5,4},{6,5},{7,6},{9,8},{10,9},{11,10},{13,12},{... | collective-permute-start | bytes 196616 | tf_op jit(solution)/shard_map/ppermute | solution.py:19
  126.7 10.8 %collective-permute-start.7 = (bf16[1,128,256]{2,1,0:T(8,128)(2,1)S(1)}, bf16[1,128,256]{2,1,0:T(8,128)(2,1)S(1)}, u32[]{:S(2)}, u32[]{:S(2)}) collective-permute-start(bf16[1,128,256]{2,1,0:T(8,128)(2,1)S(1)} %get-tuple-element.16), channel_id=1, source_target_pairs={{0,4},{4,8},{8,12},{12,16},{16,20},{20,24},{24,28},{1,5},{5,9},{9,... | collective-permute-start | bytes 196616 | tf_op jit(solution)/shard_map/ppermute | solution.py:17
  128.9 8.6 %collective-permute-start.9 = (bf16[1,128,256]{2,1,0:T(8,128)(2,1)S(1)}, bf16[1,128,256]{2,1,0:T(8,128)(2,1)S(1)}, u32[]{:S(2)}, u32[]{:S(2)}) collective-permute-start(bf16[1,128,256]{2,1,0:T(8,128)(2,1)S(1)} %get-tuple-element.17), channel_id=1, source_target_pairs={{0,1},{1,2},{2,3},{4,5},{5,6},{6,7},{8,9},{9,10},{10,11},{12,13},{... | collective-permute-start | bytes 196616 | tf_op jit(solution)/shard_map/ppermute | solution.py:17
  131.0 6.6 %collective-permute-start.8 = (bf16[1,128,256]{2,1,0:T(8,128)(2,1)S(1)}, bf16[1,128,256]{2,1,0:T(8,128)(2,1)S(1)}, u32[]{:S(2)}, u32[]{:S(2)}) collective-permute-start(bf16[1,128,256]{2,1,0:T(8,128)(2,1)S(1)} %get-tuple-element.18), channel_id=1, source_target_pairs={{4,0},{8,4},{12,8},{16,12},{20,16},{24,20},{28,24},{5,1},{9,5},{13... | collective-permute-start | bytes 196616 | tf_op jit(solution)/shard_map/ppermute | solution.py:19
  135.0 5.6 %collective-permute-start.10 = (bf16[1,128,256]{2,1,0:T(8,128)(2,1)S(1)}, bf16[1,128,256]{2,1,0:T(8,128)(2,1)S(1)}, u32[]{:S(2)}, u32[]{:S(2)}) collective-permute-start(bf16[1,128,256]{2,1,0:T(8,128)(2,1)S(1)} %get-tuple-element.19), channel_id=1, source_target_pairs={{1,0},{2,1},{3,2},{5,4},{6,5},{7,6},{9,8},{10,9},{11,10},{13,12},{... | collective-permute-start | bytes 196616 | tf_op jit(solution)/shard_map/ppermute | solution.py:19
  157.1 73.8 %copy-start.2 = (f32[256,1024]{1,0:T(8,128)S(1)}, f32[256,1024]{1,0:T(8,128)}, u32[]{:S(2)}) copy-start(f32[256,1024]{1,0:T(8,128)} %convolution_add_fusion.2) | copy-start | bytes 3145732
  157.1 18.8 %collective-permute-start.11 = (f32[768,256]{0,1:T(8,128)S(1)}, f32[768,256]{0,1:T(8,128)S(1)}, u32[]{:S(2)}, u32[]{:S(2)}) collective-permute-start(f32[768,256]{0,1:T(8,128)S(1)} %convolution_bitcast_fusion.4), channel_id=1, source_target_pairs={{0,4},{4,0},{8,12},{12,8},{16,20},{20,16},{24,28},{28,24},{1,5},{5... | collective-permute-start | bytes 2359304 | tf_op jit(solution)/shard_map/ppermute | solution.py:63
  176.0 18.0 %collective-permute-start.12 = (f32[768,256]{0,1:T(8,128)S(1)}, f32[768,256]{0,1:T(8,128)S(1)}, u32[]{:S(2)}, u32[]{:S(2)}) collective-permute-start(f32[768,256]{0,1:T(8,128)S(1)} %add.77), channel_id=1, source_target_pairs={{0,8},{4,12},{8,0},{12,4},{16,24},{20,28},{24,16},{28,20},{1,9},{5... | collective-permute-start | bytes 2359304 | tf_op jit(solution)/shard_map/ppermute | solution.py:63
  194.1 36.8 %collective-permute-start.13 = (f32[768,256]{0,1:T(8,128)S(1)}, f32[768,256]{0,1:T(8,128)S(1)}, u32[]{:S(2)}, u32[]{:S(2)}) collective-permute-start(f32[768,256]{0,1:T(8,128)S(1)} %add.78), channel_id=1, source_target_pairs={{0,16},{4,20},{8,24},{12,28},{16,0},{20,4},{24,8},{28,12},{1,17},{... | collective-permute-start | bytes 2359304 | tf_op jit(solution)/shard_map/ppermute | solution.py:63
  237.9 12.8 %collective-permute-start.14 = (bf16[1,128,256]{2,1,0:T(8,128)(2,1)S(1)}, bf16[1,128,256]{2,1,0:T(8,128)(2,1)S(1)}, u32[]{:S(2)}, u32[]{:S(2)}) collective-permute-start(bf16[1,128,256]{2,1,0:T(8,128)(2,1)S(1)} %get-tuple-element.12), channel_id=1, source_target_pairs={{0,4},{4,8},{8,12},{12,16},{16,20},{20,24},{24,28},{1,5},{5,9},{9,... | collective-permute-start | bytes 196616 | tf_op jit(solution)/shard_map/ppermute | solution.py:17
  239.8 10.9 %collective-permute-start.16 = (bf16[1,128,256]{2,1,0:T(8,128)(2,1)S(1)}, bf16[1,128,256]{2,1,0:T(8,128)(2,1)S(1)}, u32[]{:S(2)}, u32[]{:S(2)}) collective-permute-start(bf16[1,128,256]{2,1,0:T(8,128)(2,1)S(1)} %get-tuple-element.13), channel_id=1, source_target_pairs={{0,1},{1,2},{2,3},{4,5},{5,6},{6,7},{8,9},{9,10},{10,11},{12,13},{... | collective-permute-start | bytes 196616 | tf_op jit(solution)/shard_map/ppermute | solution.py:17
  244.5 6.2 %collective-permute-start.15 = (bf16[1,128,256]{2,1,0:T(8,128)(2,1)S(1)}, bf16[1,128,256]{2,1,0:T(8,128)(2,1)S(1)}, u32[]{:S(2)}, u32[]{:S(2)}) collective-permute-start(bf16[1,128,256]{2,1,0:T(8,128)(2,1)S(1)} %get-tuple-element.14), channel_id=1, source_target_pairs={{4,0},{8,4},{12,8},{16,12},{20,16},{24,20},{28,24},{5,1},{9,5},{13... | collective-permute-start | bytes 196616 | tf_op jit(solution)/shard_map/ppermute | solution.py:19
  248.7 5.6 %collective-permute-start.17 = (bf16[1,128,256]{2,1,0:T(8,128)(2,1)S(1)}, bf16[1,128,256]{2,1,0:T(8,128)(2,1)S(1)}, u32[]{:S(2)}, u32[]{:S(2)}) collective-permute-start(bf16[1,128,256]{2,1,0:T(8,128)(2,1)S(1)} %get-tuple-element.15), channel_id=1, source_target_pairs={{1,0},{2,1},{3,2},{5,4},{6,5},{7,6},{9,8},{10,9},{11,10},{13,12},{... | collective-permute-start | bytes 196616 | tf_op jit(solution)/shard_map/ppermute | solution.py:19
  271.7 13.3 %collective-permute-start.18 = (bf16[1,128,256]{2,1,0:T(8,128)(2,1)}, bf16[1,128,256]{2,1,0:T(8,128)(2,1)S(1)}, u32[]{:S(2)}, u32[]{:S(2)}) collective-permute-start(bf16[1,128,256]{2,1,0:T(8,128)(2,1)} %get-tuple-element.8), channel_id=1, source_target_pairs={{0,4},{4,8},{8,12},{12,16},{16,20},{20,24},{24,28},{1,5},{5,9},{9,... | collective-permute-start | bytes 196616 | tf_op jit(solution)/shard_map/ppermute | solution.py:17
  273.6 11.4 %collective-permute-start.20 = (bf16[1,128,256]{2,1,0:T(8,128)(2,1)}, bf16[1,128,256]{2,1,0:T(8,128)(2,1)S(1)}, u32[]{:S(2)}, u32[]{:S(2)}) collective-permute-start(bf16[1,128,256]{2,1,0:T(8,128)(2,1)} %get-tuple-element.9), channel_id=1, source_target_pairs={{0,1},{1,2},{2,3},{4,5},{5,6},{6,7},{8,9},{9,10},{10,11},{12,13},{... | collective-permute-start | bytes 196616 | tf_op jit(solution)/shard_map/ppermute | solution.py:17
  275.5 9.5 %collective-permute-start.19 = (bf16[1,128,256]{2,1,0:T(8,128)(2,1)}, bf16[1,128,256]{2,1,0:T(8,128)(2,1)S(1)}, u32[]{:S(2)}, u32[]{:S(2)}) collective-permute-start(bf16[1,128,256]{2,1,0:T(8,128)(2,1)} %get-tuple-element.10), channel_id=1, source_target_pairs={{4,0},{8,4},{12,8},{16,12},{20,16},{24,20},{28,24},{5,1},{9,5},{13... | collective-permute-start | bytes 196616 | tf_op jit(solution)/shard_map/ppermute | solution.py:19
  280.0 6.3 %collective-permute-start.21 = (bf16[1,128,256]{2,1,0:T(8,128)(2,1)S(1)}, bf16[1,128,256]{2,1,0:T(8,128)(2,1)}, u32[]{:S(2)}, u32[]{:S(2)}) collective-permute-start(bf16[1,128,256]{2,1,0:T(8,128)(2,1)S(1)} %get-tuple-element.11), channel_id=1, source_target_pairs={{1,0},{2,1},{3,2},{5,4},{6,5},{7,6},{9,8},{10,9},{11,10},{13,12},{... | collective-permute-start | bytes 196616 | tf_op jit(solution)/shard_map/ppermute | solution.py:19
  (7 other events, 134.6 us)
